TPU v7x, 32 devices: a whole 2x2x4 slice. The times are simulated.
32 devices in a mesh: sim: 2 (over y), grp: 4 (over z), gz: 4 (over x, core).
Axes of the slice: x: 2, y: 2, z: 4, core: 2. Of those that a mesh axis runs over, the one named last changes fastest.
Arguments:
- fields: float32 [8, 2, 1024, 1024], P(None, None, 'sim', ('grp', 'gz')), may hold values from -6 to 6
- diffusivity: float32 [8], replicated, may hold values from 0.03 to 0.12
- velocity: float32 [2, 8], replicated, may hold values from -0.4 to 0.4
- coupling: float32 [8, 8], replicated, may hold values from -0.6 to 0.6
- basis_x: bfloat16 [1024, 128], replicated, may hold values from -0.1875 to 0.1875
- basis_y: bfloat16 [1024, 128], replicated, may hold values from -0.1875 to 0.1875
Outputs:
- fields_out: float32 [8, 2, 1024, 1024], P(None, None, 'sim', ('grp', 'gz'))
- gram_x: float32 [1024, 1024], P('sim', ('grp', 'gz'))
- gram_y: float32 [1024, 1024], P(('grp', 'gz'), 'sim')
- core: float32 [8, 2, 128, 128], P(None, None, 'sim', ('grp', 'gz'))
All inputs are finite; a program needn't handle non-finite values.
Results may differ from a plain program's by a relative error of at most 0.0003.
Values sent between devices are 32-bit elements; how exact they have to be, the bound alone decides.
No kernel may reach another device: no remote copies, remote signals or barrier semaphores. Data moves between devices by JAX's collectives and lax.ppermute only.
A program may use at most 64 MiB of HBM per device.

v0:
```python
import jax
import jax.numpy as jnp
from jax import lax
from jax.sharding import PartitionSpec as P

NY = 1024
RANK = 128
STEPS = 2
time_step = 1.0
highest = lax.Precision.HIGHEST


def with_halo(cells, sides, width):
    for axis, dim in sides:
        count = lax.axis_size(axis)
        head = lax.slice_in_dim(cells, 0, width, axis=dim)
        tail = lax.slice_in_dim(cells, cells.shape[dim] - width, cells.shape[dim], axis=dim)
        cells = jnp.concatenate(
            [
                lax.ppermute(tail, axis, [(i, (i + 1) % count) for i in range(count)]),
                cells,
                lax.ppermute(head, axis, [((i + 1) % count, i) for i in range(count)]),
            ],
            axis=dim,
        )
    return cells


def rates(state, diffusivity, velocity, coupling):
    padded = with_halo(state, (("sim", 2), (("grp", "gz"), 3)), 1)
    center = padded[:, :, 1:-1, 1:-1]
    x_plus = padded[:, :, 2:, 1:-1]
    x_minus = padded[:, :, :-2, 1:-1]
    y_plus = padded[:, :, 1:-1, 2:]
    y_minus = padded[:, :, 1:-1, :-2]
    z_plus = jnp.roll(center, -1, 1)
    z_minus = jnp.roll(center, 1, 1)
    lapl = -6.0 * center + z_plus + z_minus + x_plus + x_minus + y_plus + y_minus
    grad_x = (x_plus - x_minus) * 0.5
    grad_y = (y_plus - y_minus) * 0.5
    react = jnp.einsum("fg,gzxy->fzxy", coupling, jnp.tanh(center), precision=highest)
    return (
        diffusivity[:, None, None, None] * lapl
        - velocity[0][:, None, None, None] * grad_x
        - velocity[1][:, None, None, None] * grad_y
        + react
    )


def shards(fields, diffusivity, velocity, coupling, basis_x, basis_y):
    state = fields
    for repeat in range(STEPS):
        first = rates(state, diffusivity, velocity, coupling)
        second = rates(state + 0.5 * time_step * first, diffusivity, velocity, coupling)
        third = rates(state + 0.5 * time_step * second, diffusivity, velocity, coupling)
        fourth = rates(state + time_step * third, diffusivity, velocity, coupling)
        state = state + time_step / 6.0 * (first + 2.0 * second + 2.0 * third + fourth)
    nfield = state.shape[0]
    depth = state.shape[1]
    x_rows = state.shape[2]
    basis_xf = basis_x.astype(jnp.float32)
    basis_yf = basis_y.astype(jnp.float32)
    block = jnp.einsum(
        "fzxy,fzwy->xw", state, lax.all_gather(state, "sim", axis=2, tiled=True), precision=highest
    )
    gram_rows = block
    own_basis = lax.dynamic_slice_in_dim(basis_xf, lax.axis_index("sim") * x_rows, x_rows, 0)
    partial_proj = jnp.einsum("xr,fzxy->fzry", own_basis, state, precision=highest)
    projected = lax.psum_scatter(partial_proj, "sim", scatter_dimension=2, tiled=True)
    gram_x = lax.psum_scatter(gram_rows, ("grp", "gz"), scatter_dimension=1, tiled=True) / (
        nfield * depth * NY
    )
    rank_grp = RANK // lax.axis_size(("grp", "gz"))
    rank_cols_y = lax.dynamic_slice_in_dim(
        basis_yf, lax.axis_index(("grp", "gz")) * rank_grp, rank_grp, 1
    )
    incoming = lax.all_gather(projected, ("grp", "gz"), axis=3, tiled=True)
    block = jnp.einsum("fzry,fzrv->yv", projected, incoming, precision=highest)
    core_part = jnp.einsum("vs,fzrv->fzrs", rank_cols_y, incoming, precision=highest)
    gram_y = lax.psum_scatter(block, "sim", scatter_dimension=1, tiled=True) / (
        nfield * depth * RANK
    )
    return (state, gram_x, gram_y, core_part)


def solution(mesh):
    in_specs = (P(None, None, "sim", ("grp", "gz")), P(), P(), P(), P(), P())
    out_specs = (
        P(None, None, "sim", ("grp", "gz")),
        P("sim", ("grp", "gz")),
        P(("grp", "gz"), "sim"),
        P(None, None, "sim", ("grp", "gz")),
    )
    return jax.shard_map(shards, mesh=mesh, in_specs=in_specs, out_specs=out_specs, check_vma=False)
```

profile of v0, /device:TPU:0, one launch (start us, length us, event | category | flops | bytes accessed | tf_op | source)
XLA Modules:
  0.0 532.1 jit_solution(15932883289345783442)
XLA Ops:
  7.2 2.8 copy.61
  10.3 3.1 collective-permute-start
  13.6 12.5 %collective-permute-done = f32[8,2,1,64]{2,0,3,1:T(8,128)S(1)} collective-permute-done((f32[8,2,1,64]{2,0,3,1:T(8,128)S(1)}, f32[8,2,1,64]{2,0,3,1:T(8,128)S(1)}, u32[]{:S(2)}, u32[]{:S(2)}) %collective-permute-start) | collective-permute-done | bytes 4128 | tf_op jit(solution)/shard_map/ppermute | solution.py:22
  26.1 10.4 %collective-permute-done.1 = f32[8,2,1,64]{2,0,3,1:T(8,128)S(1)} collective-permute-done((f32[8,2,1,64]{2,0,3,1:T(8,128)S(1)}, f32[8,2,1,64]{2,0,3,1:T(8,128)S(1)}, u32[]{:S(2)}, u32[]{:S(2)}) %collective-permute-start.1) | collective-permute-done | bytes 4128 | tf_op jit(solution)/shard_map/ppermute | solution.py:20
  36.6 3.4 collective-permute-start.2
  41.6 4.4 collective-permute-done.3
  46.1 5.2 multiply_add_fusion.3
  51.5 1.6 collective-permute-start.4
  53.6 12.5 %collective-permute-done.4 = f32[8,2,1,64]{2,0,3,1:T(8,128)S(1)} collective-permute-done((f32[8,2,1,64]{2,0,3,1:T(8,128)S(1)}, f32[8,2,1,64]{2,0,3,1:T(8,128)S(1)}, u32[]{:S(2)}, u32[]{:S(2)}) %collective-permute-start.4) | collective-permute-done | bytes 4128 | tf_op jit(solution)/shard_map/ppermute | solution.py:22
  66.1 5.6 %collective-permute-done.5 = f32[8,2,1,64]{2,0,3,1:T(8,128)S(1)} collective-permute-done((f32[8,2,1,64]{2,0,3,1:T(8,128)S(1)}, f32[8,2,1,64]{2,0,3,1:T(8,128)S(1)}, u32[]{:S(2)}, u32[]{:S(2)}) %collective-permute-start.5) | collective-permute-done | bytes 4128 | tf_op jit(solution)/shard_map/ppermute | solution.py:20
  71.9 4.1 collective-permute-start.6
  77.7 4.6 collective-permute-done.7
  82.3 4.5 multiply_add_fusion.2
  87.0 1.6 collective-permute-start.8
  89.1 12.5 %collective-permute-done.8 = f32[8,2,1,64]{2,0,3,1:T(8,128)S(1)} collective-permute-done((f32[8,2,1,64]{2,0,3,1:T(8,128)S(1)}, f32[8,2,1,64]{2,0,3,1:T(8,128)S(1)}, u32[]{:S(2)}, u32[]{:S(2)}) %collective-permute-start.8) | collective-permute-done | bytes 4128 | tf_op jit(solution)/shard_map/ppermute | solution.py:22
  101.6 5.6 %collective-permute-done.9 = f32[8,2,1,64]{2,0,3,1:T(8,128)S(1)} collective-permute-done((f32[8,2,1,64]{2,0,3,1:T(8,128)S(1)}, f32[8,2,1,64]{2,0,3,1:T(8,128)S(1)}, u32[]{:S(2)}, u32[]{:S(2)}) %collective-permute-start.9) | collective-permute-done | bytes 4128 | tf_op jit(solution)/shard_map/ppermute | solution.py:20
  107.3 2.7 collective-permute-start.10
  110.2 1.5 collective-permute-done.10
  111.7 4.4 collective-permute-done.11
  116.1 4.9 copy_add_fusion
  121.2 1.6 collective-permute-start.12
  123.3 12.5 %collective-permute-done.12 = f32[8,2,1,64]{2,0,3,1:T(8,128)S(1)} collective-permute-done((f32[8,2,1,64]{2,0,3,1:T(8,128)S(1)}, f32[8,2,1,64]{2,0,3,1:T(8,128)S(1)}, u32[]{:S(2)}, u32[]{:S(2)}) %collective-permute-start.12) | collective-permute-done | bytes 4128 | tf_op jit(solution)/shard_map/ppermute | solution.py:22
  135.8 5.6 %collective-permute-done.13 = f32[8,2,1,64]{2,0,3,1:T(8,128)S(1)} collective-permute-done((f32[8,2,1,64]{2,0,3,1:T(8,128)S(1)}, f32[8,2,1,64]{2,0,3,1:T(8,128)S(1)}, u32[]{:S(2)}, u32[]{:S(2)}) %collective-permute-start.13) | collective-permute-done | bytes 4128 | tf_op jit(solution)/shard_map/ppermute | solution.py:20
  144.5 4.6 collective-permute-done.15
  149.2 5.1 fusion.36
  154.5 1.6 collective-permute-start.16
  156.6 12.5 %collective-permute-done.16 = f32[8,2,1,64]{2,0,3,1:T(8,128)S(1)} collective-permute-done((f32[8,2,1,64]{2,0,3,1:T(8,128)S(1)}, f32[8,2,1,64]{2,0,3,1:T(8,128)S(1)}, u32[]{:S(2)}, u32[]{:S(2)}) %collective-permute-start.16) | collective-permute-done | bytes 4128 | tf_op jit(solution)/shard_map/ppermute | solution.py:22
  169.1 5.6 %collective-permute-done.17 = f32[8,2,1,64]{2,0,3,1:T(8,128)S(1)} collective-permute-done((f32[8,2,1,64]{2,0,3,1:T(8,128)S(1)}, f32[8,2,1,64]{2,0,3,1:T(8,128)S(1)}, u32[]{:S(2)}, u32[]{:S(2)}) %collective-permute-start.17) | collective-permute-done | bytes 4128 | tf_op jit(solution)/shard_map/ppermute | solution.py:20
  176.0 1.5 collective-permute-done.18
  177.5 4.4 collective-permute-done.19
  181.9 5.4 %multiply_add_fusion.1 = (f32[8,2,512,64]{2,0,3,1:T(8,128)S(1)}, f32[8,2,512,64]{2,0,3,1:T(8,128)}) fusion(f32[8,2,512,64]{2,0,3,1:T(8,128)S(1)} %fusion.36, f32[8,8]{1,0:T(8,128)S(1)} %copy-done.9, f32[8]{0:T(128)S(1)} %get-tuple-element.65, f32[8]{0:T(128)S(1)} %get-tuple-element.64, f32[8,2,1,64]{2,0,3,1:T(8,128)S(1)} %collective-permute-done.16, ...), kind=kOutput, calls=%fused_computation.154 | convolution fusion | flops 63963136 | bytes 8462944 | tf_op jit(solution)/shard_map/fg,gzxy->fzxy/dot_general | solution.py:41
  187.5 1.6 collective-permute-start.20
  189.6 12.5 %collective-permute-done.20 = f32[8,2,1,64]{2,0,3,1:T(8,128)S(1)} collective-permute-done((f32[8,2,1,64]{2,0,3,1:T(8,128)S(1)}, f32[8,2,1,64]{2,0,3,1:T(8,128)S(1)}, u32[]{:S(2)}, u32[]{:S(2)}) %collective-permute-start.20) | collective-permute-done | bytes 4128 | tf_op jit(solution)/shard_map/ppermute | solution.py:22
  202.1 5.6 %collective-permute-done.21 = f32[8,2,1,64]{2,0,3,1:T(8,128)S(1)} collective-permute-done((f32[8,2,1,64]{2,0,3,1:T(8,128)S(1)}, f32[8,2,1,64]{2,0,3,1:T(8,128)S(1)}, u32[]{:S(2)}, u32[]{:S(2)}) %collective-permute-start.21) | collective-permute-done | bytes 4128 | tf_op jit(solution)/shard_map/ppermute | solution.py:20
  209.2 1.5 collective-permute-done.22
  210.7 4.4 collective-permute-done.23
  215.1 5.5 %multiply_add_fusion = (f32[8,2,512,64]{2,0,3,1:T(8,128)S(1)}, f32[8,2,512,64]{2,0,3,1:T(8,128)}) fusion(f32[8,2,512,64]{2,0,3,1:T(8,128)S(1)} %fusion.36, f32[8,8]{1,0:T(8,128)S(1)} %copy-done.9, f32[8,2,512,64]{2,0,3,1:T(8,128)S(1)} %get-tuple-element.72, f32[8]{0:T(128)S(1)} %get-tuple-element.65, f32[8]{0:T(128)S(1)} %get-tuple-element.64, ...), kind=kOutput, calls=%fused_computation.151 | convolution fusion | flops 63963136 | bytes 10560096 | tf_op jit(solution)/shard_map/fg,gzxy->fzxy/dot_general | solution.py:41
  220.9 1.6 collective-permute-start.24
  223.0 12.5 %collective-permute-done.24 = f32[8,2,1,64]{2,0,3,1:T(8,128)S(1)} collective-permute-done((f32[8,2,1,64]{2,0,3,1:T(8,128)S(1)}, f32[8,2,1,64]{2,0,3,1:T(8,128)S(1)}, u32[]{:S(2)}, u32[]{:S(2)}) %collective-permute-start.24) | collective-permute-done | bytes 4128 | tf_op jit(solution)/shard_map/ppermute | solution.py:22
  235.5 5.6 %collective-permute-done.25 = f32[8,2,1,64]{2,0,3,1:T(8,128)S(1)} collective-permute-done((f32[8,2,1,64]{2,0,3,1:T(8,128)S(1)}, f32[8,2,1,64]{2,0,3,1:T(8,128)S(1)}, u32[]{:S(2)}, u32[]{:S(2)}) %collective-permute-start.25) | collective-permute-done | bytes 4128 | tf_op jit(solution)/shard_map/ppermute | solution.py:20
  241.2 1.9 collective-permute-start.26
  244.8 4.8 collective-permute-done.27
  249.7 5.6 %fusion.158 = (f32[8,2,512,64]{2,0,3,1:T(8,128)S(1)}, f32[8,2,512,64]{2,0,3,1:T(8,128)}) fusion(f32[8,2,512,64]{2,0,3,1:T(8,128)S(1)} %fusion.36, f32[8,8]{1,0:T(8,128)S(1)} %copy-done.9, f32[8,2,512,64]{2,0,3,1:T(8,128)S(1)} %get-tuple-element.74, f32[8]{0:T(128)S(1)} %get-tuple-element.65, f32[8]{0:T(128)S(1)} %get-tuple-element.64, ...), kind=kOutput, calls=%fused_computation.229 | convolution fusion | flops 63438848 | bytes 10560096 | tf_op jit(solution)/shard_map/fg,gzxy->fzxy/dot_general | solution.py:41
  256.6 1.5 collective-permute-start.28
  258.7 12.7 %collective-permute-done.28 = f32[8,2,1,64]{2,0,3,1:T(8,128)S(1)} collective-permute-done((f32[8,2,1,64]{2,0,3,1:T(8,128)}, f32[8,2,1,64]{2,0,3,1:T(8,128)S(1)}, u32[]{:S(2)}, u32[]{:S(2)}) %collective-permute-start.28) | collective-permute-done | bytes 4128 | tf_op jit(solution)/shard_map/ppermute | solution.py:22
  271.4 5.6 %collective-permute-done.29 = f32[8,2,1,64]{2,0,3,1:T(8,128)S(1)} collective-permute-done((f32[8,2,1,64]{2,0,3,1:T(8,128)}, f32[8,2,1,64]{2,0,3,1:T(8,128)S(1)}, u32[]{:S(2)}, u32[]{:S(2)}) %collective-permute-start.29) | collective-permute-done | bytes 4128 | tf_op jit(solution)/shard_map/ppermute | solution.py:20
  277.1 1.8 collective-permute-start.30
  280.5 4.5 collective-permute-done.31
  285.0 8.8 %fusion.71 = f32[8,2,512,64]{2,0,3,1:T(8,128)S(1)} fusion(f32[8,2,512,64]{2,0,3,1:T(8,128)S(1)} %copy-done.4, f32[8,1,512,64]{2,0,3,1:T(8,128)S(1)} %get-tuple-element.35, f32[8,1,512,64]{2,0,3,1:T(8,128)S(1)} %get-tuple-element.34, f32[8,2,514,1]{2,0,3,1:T(8,128)S(1)} %collective-permute-done.30, f32[8,2,1,64]{2,0,3,1:T(8,128)S(1)} %collective-permute-done.28, ...), kind=kOutput, calls=%fused_computation.79 | convolution fusion | flops 66584576 | bytes 14754400 | tf_op jit(solution)/shard_map/fg,gzxy->fzxy/dot_general | solution.py:41
  293.9 1.9 convolution_bitcast_fusion
  295.8 1.9 copy.75
  297.7 1.8 reshape.20
  300.3 11.4 %reduce-scatter.10.cloned.1.call-done = f32[64,1024]{1,0:T(8,128)} async-done(((f32[128,1024]{1,0:T(8,128)}), f32[64,1024]{1,0:T(8,128)}) %reduce-scatter.10.cloned.1.call-update) | async-done | bytes 262160
  314.5 56.1 %all-gather.3.cloned.1.call-done = f32[8,2,1024,64]{2,0,3,1:T(8,128)} async-done(((f32[8,2,512,64]{2,0,3,1:T(8,128)}), f32[8,2,1024,64]{2,0,3,1:T(8,128)}) %all-gather.3.cloned.1.call-update) | async-done | bytes 4194320 | tf_op jit(solution)/shard_map/all_gather | solution.py:64
  370.5 9.7 %fusion.89 = f32[512,1024]{0,1:T(8,128)} fusion(f32[8,2,1024,64]{2,0,3,1:T(8,128)} %all-gather.3.cloned.1.call-done, f32[8,2,512,64]{2,0,3,1:T(8,128)S(1)} %copy-done.2), kind=kOutput, calls=%fused_computation.165 | convolution fusion | flops 6442450944 | bytes 8388608 | tf_op jit(solution)/shard_map/fzxy,fzwy->xw/dot_general | solution.py:63
  380.3 2.5 copy.69
  382.8 64.2 %all-gather.5.cloned.1.call-done = f32[8,2,64,1024]{2,0,1,3:T(8,128)} async-done(((f32[8,2,64,64]{2,0,1,3:T(8,128)}), f32[8,2,64,1024]{2,0,1,3:T(8,128)}) %all-gather.5.cloned.1.call-update) | async-done | bytes 4194320 | tf_op jit(solution)/shard_map/all_gather | solution.py:77
  447.0 6.9 %copy.66 = f32[8,2,64,1024]{3,2,1,0:T(8,128)} copy(f32[8,2,64,1024]{2,0,1,3:T(8,128)} %all-gather.5.cloned.1.call-done) | data formatting | bytes 8388608 | tf_op jit(solution)/shard_map/all_gather | solution.py:77
  453.9 5.8 %convolution_bitcast_fusion.1 = f32[64,1024]{1,0:T(8,128)} fusion(f32[8,2,64,1024]{3,2,1,0:T(8,128)} %copy.66, f32[8,2,64,64]{3,1,0,2:T(2,128)S(1)} %bitcast.93), kind=kOutput, calls=%fused_computation.167 | convolution fusion | flops 805306368 | bytes 4718592 | tf_op jit(solution)/shard_map/fzry,fzrv->yv/dot_general | solution.py:78
  459.7 51.4 %reduce-scatter.6.cloned.1.call-done = f32[512,64]{0,1:T(8,128)} async-done(((f32[512,1024]{0,1:T(8,128)}), f32[512,64]{0,1:T(8,128)}) %reduce-scatter.6.cloned.1.call-update) | async-done | bytes 131088 | tf_op jit(solution)/shard_map/reduce_scatter | solution.py:70
  511.0 1.6 broadcast_multiply_fusion.1
  512.6 5.5 %fusion.95 = f32[8,2,64,8]{2,3,1,0:T(8,128)} fusion(f32[8,2,64,1024]{3,2,1,0:T(8,128)} %copy.66, bf16[1024,128]{1,0:T(8,128)(2,1)S(1)} %copy-done.7, s32[]{:T(128)S(6)} %select_n.7), kind=kOutput, calls=%fused_computation.169 | convolution fusion | flops 100663296 | bytes 4489220 | tf_op jit(solution)/shard_map/vs,fzrv->fzrs/dot_general | solution.py:79
  518.0 5.8 %reduce-scatter.8.cloned.1.call-done = f32[64,512]{1,0:T(8,128)} async-done(((f32[64,1024]{1,0:T(8,128)}), f32[64,512]{1,0:T(8,128)}) %reduce-scatter.8.cloned.1.call-update) | async-done | bytes 131088 | tf_op jit(solution)/shard_map/reduce_scatter | solution.py:80
  523.8 1.6 broadcast_multiply_fusion
  (88 shorter events, 23.2 us)
Async XLA Ops:
  7.2 286.7 %copy-start = (bf16[1024,128]{1,0:T(8,128)(2,1)S(1)}, bf16[1024,128]{1,0:T(8,128)(2,1)}, u32[]{:S(2)}) copy-start(bf16[1024,128]{1,0:T(8,128)(2,1)} %param.10) | copy-start | bytes 786436
  7.2 304.5 %reduce-scatter.10.cloned.1.call-start = ((), (), s32[]{:S(2)}) async-start(), calls=%async_computation.7 | async-start | bytes 786432
  10.3 15.8 %collective-permute-start = (f32[8,2,1,64]{2,0,3,1:T(8,128)S(1)}, f32[8,2,1,64]{2,0,3,1:T(8,128)S(1)}, u32[]{:S(2)}, u32[]{:S(2)}) collective-permute-start(f32[8,2,1,64]{2,0,3,1:T(8,128)S(1)} %get-tuple-element.61), channel_id=1, source_target_pairs={{16,0},{0,16},{17,1},{1,17},{18,2},{2,18},{19,3},{3,19},{20,4},{4,... | collective-permute-start | bytes 12296 | tf_op jit(solution)/shard_map/ppermute | solution.py:22
  13.3 23.2 %collective-permute-start.1 = (f32[8,2,1,64]{2,0,3,1:T(8,128)S(1)}, f32[8,2,1,64]{2,0,3,1:T(8,128)S(1)}, u32[]{:S(2)}, u32[]{:S(2)}) collective-permute-start(f32[8,2,1,64]{2,0,3,1:T(8,128)S(1)} %get-tuple-element.60), channel_id=1, source_target_pairs={{0,16},{16,0},{1,17},{17,1},{2,18},{18,2},{3,19},{19,3},{4,20},{20... | collective-permute-start | bytes 12296 | tf_op jit(solution)/shard_map/ppermute | solution.py:20
  13.6 26.4 %copy-start.8 = (f32[2,8]{1,0:T(2,128)S(1)}, f32[2,8]{1,0:T(2,128)}, u32[]{:S(2)}) copy-start(f32[2,8]{1,0:T(2,128)} %param.8) | copy-start | bytes 196
  13.6 26.4 %copy-start.6 = (f32[8,2,512,64]{2,3,1,0:T(8,128)S(1)}, f32[8,2,512,64]{2,3,1,0:T(8,128)}, u32[]{:S(2)}) copy-start(f32[8,2,512,64]{2,3,1,0:T(8,128)} %param.6) | copy-start | bytes 6291460
  36.6 5.1 collective-permute-start.2
  40.0 6.1 %collective-permute-start.3 = (f32[8,2,514,1]{2,0,3,1:T(8,128)S(1)}, f32[8,2,514,1]{2,0,3,1:T(8,128)S(1)}, u32[]{:S(2)}, u32[]{:S(2)}) collective-permute-start(f32[8,2,514,1]{2,0,3,1:T(8,128)S(1)} %get-tuple-element.30), channel_id=1, source_target_pairs={{0,1},{1,2},{2,3},{3,4},{4,5},{5,6},{6,7},{7,8},{8,9},{9,10},{10,1... | collective-permute-start | bytes 98696 | tf_op jit(solution)/shard_map/ppermute | solution.py:20
  40.0 6.1 %copy-start.9 = (f32[8,8]{1,0:T(8,128)S(1)}, f32[8,8]{1,0:T(8,128)}, u32[]{:S(2)}) copy-start(f32[8,8]{1,0:T(8,128)} %param.9) | copy-start | bytes 772
  40.0 6.1 %copy-start.10 = (f32[8]{0:T(128)S(1)}, f32[8]{0:T(128)}, u32[]{:S(2)}) copy-start(f32[8]{0:T(128)} %param.7) | copy-start | bytes 100
  51.5 14.6 %collective-permute-start.4 = (f32[8,2,1,64]{2,0,3,1:T(8,128)S(1)}, f32[8,2,1,64]{2,0,3,1:T(8,128)S(1)}, u32[]{:S(2)}, u32[]{:S(2)}) collective-permute-start(f32[8,2,1,64]{2,0,3,1:T(8,128)S(1)} %get-tuple-element.57), channel_id=1, source_target_pairs={{16,0},{0,16},{17,1},{1,17},{18,2},{2,18},{19,3},{3,19},{20,4},{4,... | collective-permute-start | bytes 12296 | tf_op jit(solution)/shard_map/ppermute | solution.py:22
  53.1 18.6 %collective-permute-start.5 = (f32[8,2,1,64]{2,0,3,1:T(8,128)S(1)}, f32[8,2,1,64]{2,0,3,1:T(8,128)S(1)}, u32[]{:S(2)}, u32[]{:S(2)}) collective-permute-start(f32[8,2,1,64]{2,0,3,1:T(8,128)S(1)} %get-tuple-element.56), channel_id=1, source_target_pairs={{0,16},{16,0},{1,17},{17,1},{2,18},{18,2},{3,19},{19,3},{4,20},{20... | collective-permute-start | bytes 12296 | tf_op jit(solution)/shard_map/ppermute | solution.py:20
  71.9 5.8 %collective-permute-start.6 = (f32[8,2,514,1]{2,0,3,1:T(8,128)S(1)}, f32[8,2,514,1]{2,0,3,1:T(8,128)S(1)}, u32[]{:S(2)}, u32[]{:S(2)}) collective-permute-start(f32[8,2,514,1]{2,0,3,1:T(8,128)S(1)} %get-tuple-element.29), channel_id=1, source_target_pairs={{1,0},{2,1},{3,2},{4,3},{5,4},{6,5},{7,6},{8,7},{9,8},{10,9},{11,1... | collective-permute-start | bytes 98696 | tf_op jit(solution)/shard_map/ppermute | solution.py:22
  76.0 6.3 %collective-permute-start.7 = (f32[8,2,514,1]{2,0,3,1:T(8,128)S(1)}, f32[8,2,514,1]{2,0,3,1:T(8,128)S(1)}, u32[]{:S(2)}, u32[]{:S(2)}) collective-permute-start(f32[8,2,514,1]{2,0,3,1:T(8,128)S(1)} %get-tuple-element.28), channel_id=1, source_target_pairs={{0,1},{1,2},{2,3},{3,4},{4,5},{5,6},{6,7},{7,8},{8,9},{9,10},{10,1... | collective-permute-start | bytes 98696 | tf_op jit(solution)/shard_map/ppermute | solution.py:20
  87.0 14.6 %collective-permute-start.8 = (f32[8,2,1,64]{2,0,3,1:T(8,128)S(1)}, f32[8,2,1,64]{2,0,3,1:T(8,128)S(1)}, u32[]{:S(2)}, u32[]{:S(2)}) collective-permute-start(f32[8,2,1,64]{2,0,3,1:T(8,128)S(1)} %get-tuple-element.53), channel_id=1, source_target_pairs={{16,0},{0,16},{17,1},{1,17},{18,2},{2,18},{19,3},{3,19},{20,4},{4,... | collective-permute-start | bytes 12296 | tf_op jit(solution)/shard_map/ppermute | solution.py:22
  88.6 18.6 %collective-permute-start.9 = (f32[8,2,1,64]{2,0,3,1:T(8,128)S(1)}, f32[8,2,1,64]{2,0,3,1:T(8,128)S(1)}, u32[]{:S(2)}, u32[]{:S(2)}) collective-permute-start(f32[8,2,1,64]{2,0,3,1:T(8,128)S(1)} %get-tuple-element.52), channel_id=1, source_target_pairs={{0,16},{16,0},{1,17},{17,1},{2,18},{18,2},{3,19},{19,3},{4,20},{20... | collective-permute-start | bytes 12296 | tf_op jit(solution)/shard_map/ppermute | solution.py:20
  107.3 4.3 collective-permute-start.10
  110.0 6.1 %collective-permute-start.11 = (f32[8,2,514,1]{2,0,3,1:T(8,128)S(1)}, f32[8,2,514,1]{2,0,3,1:T(8,128)S(1)}, u32[]{:S(2)}, u32[]{:S(2)}) collective-permute-start(f32[8,2,514,1]{2,0,3,1:T(8,128)S(1)} %get-tuple-element.26), channel_id=1, source_target_pairs={{0,1},{1,2},{2,3},{3,4},{4,5},{5,6},{6,7},{7,8},{8,9},{9,10},{10,1... | collective-permute-start | bytes 98696 | tf_op jit(solution)/shard_map/ppermute | solution.py:20
  121.2 14.6 %collective-permute-start.12 = (f32[8,2,1,64]{2,0,3,1:T(8,128)S(1)}, f32[8,2,1,64]{2,0,3,1:T(8,128)S(1)}, u32[]{:S(2)}, u32[]{:S(2)}) collective-permute-start(f32[8,2,1,64]{2,0,3,1:T(8,128)S(1)} %get-tuple-element.49), channel_id=1, source_target_pairs={{16,0},{0,16},{17,1},{1,17},{18,2},{2,18},{19,3},{3,19},{20,4},{4,... | collective-permute-start | bytes 12296 | tf_op jit(solution)/shard_map/ppermute | solution.py:22
  122.8 18.6 %collective-permute-start.13 = (f32[8,2,1,64]{2,0,3,1:T(8,128)S(1)}, f32[8,2,1,64]{2,0,3,1:T(8,128)S(1)}, u32[]{:S(2)}, u32[]{:S(2)}) collective-permute-start(f32[8,2,1,64]{2,0,3,1:T(8,128)S(1)} %get-tuple-element.48), channel_id=1, source_target_pairs={{0,16},{16,0},{1,17},{17,1},{2,18},{18,2},{3,19},{19,3},{4,20},{20... | collective-permute-start | bytes 12296 | tf_op jit(solution)/shard_map/ppermute | solution.py:20
  141.5 3.0 collective-permute-start.14
  142.9 6.3 %collective-permute-start.15 = (f32[8,2,514,1]{2,0,3,1:T(8,128)S(1)}, f32[8,2,514,1]{2,0,3,1:T(8,128)S(1)}, u32[]{:S(2)}, u32[]{:S(2)}) collective-permute-start(f32[8,2,514,1]{2,0,3,1:T(8,128)S(1)} %get-tuple-element.24), channel_id=1, source_target_pairs={{0,1},{1,2},{2,3},{3,4},{4,5},{5,6},{6,7},{7,8},{8,9},{9,10},{10,1... | collective-permute-start | bytes 98696 | tf_op jit(solution)/shard_map/ppermute | solution.py:20
  154.3 95.4 %copy-start.3 = (f32[8,2,512,64]{2,0,3,1:T(8,128)}, f32[8,2,512,64]{2,0,3,1:T(8,128)S(1)}, u32[]{:S(2)}) copy-start(f32[8,2,512,64]{2,0,3,1:T(8,128)S(1)} %fusion.36) | copy-start | bytes 6291460
  154.5 14.6 %collective-permute-start.16 = (f32[8,2,1,64]{2,0,3,1:T(8,128)S(1)}, f32[8,2,1,64]{2,0,3,1:T(8,128)S(1)}, u32[]{:S(2)}, u32[]{:S(2)}) collective-permute-start(f32[8,2,1,64]{2,0,3,1:T(8,128)S(1)} %get-tuple-element.45), channel_id=1, source_target_pairs={{16,0},{0,16},{17,1},{1,17},{18,2},{2,18},{19,3},{3,19},{20,4},{4,... | collective-permute-start | bytes 12296 | tf_op jit(solution)/shard_map/ppermute | solution.py:22
  156.1 18.6 %collective-permute-start.17 = (f32[8,2,1,64]{2,0,3,1:T(8,128)S(1)}, f32[8,2,1,64]{2,0,3,1:T(8,128)S(1)}, u32[]{:S(2)}, u32[]{:S(2)}) collective-permute-start(f32[8,2,1,64]{2,0,3,1:T(8,128)S(1)} %get-tuple-element.44), channel_id=1, source_target_pairs={{0,16},{16,0},{1,17},{17,1},{2,18},{18,2},{3,19},{19,3},{4,20},{20... | collective-permute-start | bytes 12296 | tf_op jit(solution)/shard_map/ppermute | solution.py:20
  174.8 2.6 collective-permute-start.18
  175.8 6.1 %collective-permute-start.19 = (f32[8,2,514,1]{2,0,3,1:T(8,128)S(1)}, f32[8,2,514,1]{2,0,3,1:T(8,128)S(1)}, u32[]{:S(2)}, u32[]{:S(2)}) collective-permute-start(f32[8,2,514,1]{2,0,3,1:T(8,128)S(1)} %get-tuple-element.22), channel_id=1, source_target_pairs={{0,1},{1,2},{2,3},{3,4},{4,5},{5,6},{6,7},{7,8},{8,9},{9,10},{10,1... | collective-permute-start | bytes 98696 | tf_op jit(solution)/shard_map/ppermute | solution.py:20
  187.5 14.6 %collective-permute-start.20 = (f32[8,2,1,64]{2,0,3,1:T(8,128)S(1)}, f32[8,2,1,64]{2,0,3,1:T(8,128)S(1)}, u32[]{:S(2)}, u32[]{:S(2)}) collective-permute-start(f32[8,2,1,64]{2,0,3,1:T(8,128)S(1)} %get-tuple-element.41), channel_id=1, source_target_pairs={{16,0},{0,16},{17,1},{1,17},{18,2},{2,18},{19,3},{3,19},{20,4},{4,... | collective-permute-start | bytes 12296 | tf_op jit(solution)/shard_map/ppermute | solution.py:22
  189.1 18.6 %collective-permute-start.21 = (f32[8,2,1,64]{2,0,3,1:T(8,128)S(1)}, f32[8,2,1,64]{2,0,3,1:T(8,128)S(1)}, u32[]{:S(2)}, u32[]{:S(2)}) collective-permute-start(f32[8,2,1,64]{2,0,3,1:T(8,128)S(1)} %get-tuple-element.40), channel_id=1, source_target_pairs={{0,16},{16,0},{1,17},{17,1},{2,18},{18,2},{3,19},{19,3},{4,20},{20... | collective-permute-start | bytes 12296 | tf_op jit(solution)/shard_map/ppermute | solution.py:20
  207.9 2.8 collective-permute-start.22
  209.0 6.1 %collective-permute-start.23 = (f32[8,2,514,1]{2,0,3,1:T(8,128)S(1)}, f32[8,2,514,1]{2,0,3,1:T(8,128)S(1)}, u32[]{:S(2)}, u32[]{:S(2)}) collective-permute-start(f32[8,2,514,1]{2,0,3,1:T(8,128)S(1)} %get-tuple-element.20), channel_id=1, source_target_pairs={{0,1},{1,2},{2,3},{3,4},{4,5},{5,6},{6,7},{7,8},{8,9},{9,10},{10,1... | collective-permute-start | bytes 98696 | tf_op jit(solution)/shard_map/ppermute | solution.py:20
  220.9 14.6 %collective-permute-start.24 = (f32[8,2,1,64]{2,0,3,1:T(8,128)S(1)}, f32[8,2,1,64]{2,0,3,1:T(8,128)S(1)}, u32[]{:S(2)}, u32[]{:S(2)}) collective-permute-start(f32[8,2,1,64]{2,0,3,1:T(8,128)S(1)} %get-tuple-element.37), channel_id=1, source_target_pairs={{16,0},{0,16},{17,1},{1,17},{18,2},{2,18},{19,3},{3,19},{20,4},{4,... | collective-permute-start | bytes 12296 | tf_op jit(solution)/shard_map/ppermute | solution.py:22
  222.5 18.6 %collective-permute-start.25 = (f32[8,2,1,64]{2,0,3,1:T(8,128)S(1)}, f32[8,2,1,64]{2,0,3,1:T(8,128)S(1)}, u32[]{:S(2)}, u32[]{:S(2)}) collective-permute-start(f32[8,2,1,64]{2,0,3,1:T(8,128)S(1)} %get-tuple-element.36), channel_id=1, source_target_pairs={{0,16},{16,0},{1,17},{17,1},{2,18},{18,2},{3,19},{19,3},{4,20},{20... | collective-permute-start | bytes 12296 | tf_op jit(solution)/shard_map/ppermute | solution.py:20
  241.2 3.6 collective-permute-start.26
  243.2 6.5 %collective-permute-start.27 = (f32[8,2,514,1]{2,0,3,1:T(8,128)S(1)}, f32[8,2,514,1]{2,0,3,1:T(8,128)S(1)}, u32[]{:S(2)}, u32[]{:S(2)}) collective-permute-start(f32[8,2,514,1]{2,0,3,1:T(8,128)S(1)} %get-tuple-element.18), channel_id=1, source_target_pairs={{0,1},{1,2},{2,3},{3,4},{4,5},{5,6},{6,7},{7,8},{8,9},{9,10},{10,1... | collective-permute-start | bytes 98696 | tf_op jit(solution)/shard_map/ppermute | solution.py:20
  255.3 23.6 %copy-start.5 = (f32[8,2,512,64]{2,0,3,1:T(8,128)}, f32[8,2,512,64]{2,0,3,1:T(8,128)S(1)}, u32[]{:S(2)}) copy-start(f32[8,2,512,64]{2,0,3,1:T(8,128)S(1)} %get-tuple-element.76) | copy-start | bytes 6291460
  256.6 14.8 %collective-permute-start.28 = (f32[8,2,1,64]{2,0,3,1:T(8,128)}, f32[8,2,1,64]{2,0,3,1:T(8,128)S(1)}, u32[]{:S(2)}, u32[]{:S(2)}) collective-permute-start(f32[8,2,1,64]{2,0,3,1:T(8,128)} %get-tuple-element.33), channel_id=1, source_target_pairs={{16,0},{0,16},{17,1},{1,17},{18,2},{2,18},{19,3},{3,19},{20,4},{4,... | collective-permute-start | bytes 12296 | tf_op jit(solution)/shard_map/ppermute | solution.py:22
  258.2 18.9 %collective-permute-start.29 = (f32[8,2,1,64]{2,0,3,1:T(8,128)}, f32[8,2,1,64]{2,0,3,1:T(8,128)S(1)}, u32[]{:S(2)}, u32[]{:S(2)}) collective-permute-start(f32[8,2,1,64]{2,0,3,1:T(8,128)} %get-tuple-element.32), channel_id=1, source_target_pairs={{0,16},{16,0},{1,17},{17,1},{2,18},{18,2},{3,19},{19,3},{4,20},{20... | collective-permute-start | bytes 12296 | tf_op jit(solution)/shard_map/ppermute | solution.py:20
  277.0 8.0 %copy-start.12 = (f32[8,2,512,64]{2,0,3,1:T(8,128)S(1)}, f32[8,2,512,64]{2,0,3,1:T(8,128)}, u32[]{:S(2)}) copy-start(f32[8,2,512,64]{2,0,3,1:T(8,128)} %get-tuple-element.75) | copy-start | bytes 6291460
  277.1 3.4 collective-permute-start.30
  278.9 6.1 %copy-start.4 = (f32[8,2,512,64]{2,0,3,1:T(8,128)S(1)}, f32[8,2,512,64]{2,0,3,1:T(8,128)}, u32[]{:S(2)}) copy-start(f32[8,2,512,64]{2,0,3,1:T(8,128)} %copy-done.3) | copy-start | bytes 6291460
  278.9 6.1 %copy-start.11 = (f32[8,2,512,64]{2,0,3,1:T(8,128)S(1)}, f32[8,2,512,64]{2,0,3,1:T(8,128)}, u32[]{:S(2)}) copy-start(f32[8,2,512,64]{2,0,3,1:T(8,128)} %get-tuple-element.73) | copy-start | bytes 6291460
  278.9 6.1 %collective-permute-start.31 = (f32[8,2,514,1]{2,0,3,1:T(8,128)S(1)}, f32[8,2,514,1]{2,0,3,1:T(8,128)S(1)}, u32[]{:S(2)}, u32[]{:S(2)}) collective-permute-start(f32[8,2,514,1]{2,0,3,1:T(8,128)S(1)} %get-tuple-element.16), channel_id=1, source_target_pairs={{0,1},{1,2},{2,3},{3,4},{4,5},{5,6},{6,7},{7,8},{8,9},{9,10},{10,1... | collective-permute-start | bytes 98696 | tf_op jit(solution)/shard_map/ppermute | solution.py:20
  293.8 3.8 copy-start.1
  299.5 71.0 %copy-start.2 = (f32[8,2,512,64]{2,0,3,1:T(8,128)S(1)}, f32[8,2,512,64]{2,0,3,1:T(8,128)}, u32[]{:S(2)}) copy-start(f32[8,2,512,64]{2,0,3,1:T(8,128)} %copy-done.1) | copy-start | bytes 6291460
  299.5 71.0 %all-gather.3.cloned.1.call-start = ((), (), s32[]{:S(2)}) async-start(), calls=%async_computation.3 | async-start | bytes 6291456 | tf_op jit(solution)/shard_map/all_gather | solution.py:64
  300.2 146.8 %all-gather.5.cloned.1.call-start = ((), (), s32[]{:S(2)}) async-start(), calls=%async_computation.5 | async-start | bytes 8912896 | tf_op jit(solution)/shard_map/all_gather | solution.py:77
  314.2 196.8 %reduce-scatter.6.cloned.1.call-start = ((), (), s32[]{:S(2)}) async-start(), calls=%async_computation.4 | async-start | bytes 2228224 | tf_op jit(solution)/shard_map/reduce_scatter | solution.py:70
  380.2 143.6 %reduce-scatter.8.cloned.1.call-start = ((), (), s32[]{:S(2)}) async-start(), calls=%async_computation.6 | async-start | bytes 393216 | tf_op jit(solution)/shard_map/reduce_scatter | solution.py:80
  453.9 58.7 %copy-start.7 = (bf16[1024,128]{1,0:T(8,128)(2,1)S(1)}, bf16[1024,128]{1,0:T(8,128)(2,1)}, u32[]{:S(2)}) copy-start(bf16[1024,128]{1,0:T(8,128)(2,1)} %param.11) | copy-start | bytes 786436
Sparse Core Ops, SparseCore 0:
  299.6 11.9 reduce-scatter.9
  313.8 56.7 all-gather.2
  372.7 74.2 all-gather.4
  450.6 60.3 reduce-scatter.5
  513.1 10.6 reduce-scatter.7
where the time goes:
time: 539 us; the launch traced here: 532 us
  waiting for transfers between devices  387 us (72%)
  matrix products  68 us (13%)
  starting transfers between devices  36.2 us (7%)
  local copies, waits for them, and re-layouts  23 us (4%)
  between operations  14.3 us (3%)
    ppermute x16, waiting for transfers between devices, with_halo(): lax.ppermute(head, axis, [((i + 1) % count, i) for i in range(count)])  111 us
    ppermute x16, waiting for transfers between devices, with_halo(): lax.ppermute(tail, axis, [(i, (i + 1) % count) for i in range(count)])  86 us
    all_gather x1, waiting for transfers between devices, shards(): incoming = lax.all_gather(projected, ('grp', 'gz'), axis=3, tiled=True)  64.2 us
    all_gather x1, waiting for transfers between devices, shards(): lax.all_gather(state, 'sim', axis=2, tiled=True)  56.1 us
    reduce_scatter x1, waiting for transfers between devices, shards(): lax.psum_scatter(gram_rows, ('grp', 'gz'), scatter_dimension=1, tiled=True)  51.4 us
    dot_general x8, matrix products, rates(): jnp.einsum('fg,gzxy->fzxy', coupling, jnp.tanh(center), precision=highest)  45.2 us
    ppermute x16, starting transfers between devices, with_halo(): lax.ppermute(head, axis, [((i + 1) % count, i) for i in range(count)])  31.4 us
    unnamed x6, waiting for transfers between devices  12.1 us
  transfers between devices with their start and end apart: 37, of which 37 were waited for; matrix products, arithmetic and copies ran while one was open for 7% of the time, Pallas kernels for 0%

commit v1 on v0

--- a/solution.py
+++ b/solution.py
@@ -60,9 +60,21 @@
     x_rows = state.shape[2]
     basis_xf = basis_x.astype(jnp.float32)
     basis_yf = basis_y.astype(jnp.float32)
-    block = jnp.einsum(
-        "fzxy,fzwy->xw", state, lax.all_gather(state, "sim", axis=2, tiled=True), precision=highest
-    )
+    count_2, here, span = (lax.axis_size("sim"), lax.axis_index("sim"), state.shape[2])
+    forward = [(i_2, (i_2 + 1) % count_2) for i_2 in range(count_2)]
+    block_2, result = (state, None)
+    for hop in range(count_2):
+        owner = (here - hop) % count_2
+        coming = lax.ppermute(block_2, "sim", forward) if hop < count_2 - 1 else None
+        made = jnp.einsum("fzxy,fzwy->xw", state, block_2, precision=highest)
+        length = made.shape[1]
+        if result is None:
+            result = jnp.zeros(
+                (*made.shape[:1], count_2 * length, *made.shape[1 + 1 :]), made.dtype
+            )
+        result = lax.dynamic_update_slice_in_dim(result, made, owner * length, axis=1)
+        block_2 = coming
+    block = result
     gram_rows = block
     own_basis = lax.dynamic_slice_in_dim(basis_xf, lax.axis_index("sim") * x_rows, x_rows, 0)
     partial_proj = jnp.einsum("xr,fzxy->fzry", own_basis, state, precision=highest)

time: 539 us -> 480 us (0.89)
  waiting for transfers between devices: 387 us -> 326 us
    all_gather x1 -> x0, waiting for transfers between devices: 56.1 us -> none  [shards(): lax.all_gather(state, 'sim', axis=2, tiled=True)]
    all_gather x1, waiting for transfers between devices: 64.2 us -> 17.9 us  [shards(): incoming = lax.all_gather(projected, ('grp', 'gz'), axis=3, tiled=True)]
    ppermute x0 -> x1, waiting for transfers between devices: none -> 40.9 us  [shards(): lax.ppermute(block_2, 'sim', forward)]
    unnamed x6 -> x5, waiting for transfers between devices: 12.1 us -> 12.2 us
  transfers between devices with their start and end apart: 37 -> 37, of which waited for: 37 -> 37; matrix products, arithmetic and copies ran while one was open for 7% -> 8% of each run, Pallas kernels for 0% -> 0%
where the time goes in v1:
time: 480 us; the launch traced here: 474 us
  waiting for transfers between devices  326 us (68%)
  matrix products  69 us (14%)
  starting transfers between devices  36.7 us (8%)
  local copies, waits for them, and re-layouts  24.4 us (5%)
  between operations  14.3 us (3%)
    ppermute x16, waiting for transfers between devices, with_halo(): lax.ppermute(head, axis, [((i + 1) % count, i) for i in range(count)])  111 us
    ppermute x16, waiting for transfers between devices, with_halo(): lax.ppermute(tail, axis, [(i, (i + 1) % count) for i in range(count)])  86 us
    reduce_scatter x1, waiting for transfers between devices, shards(): lax.psum_scatter(gram_rows, ('grp', 'gz'), scatter_dimension=1, tiled=True)  51.5 us
    dot_general x8, matrix products, rates(): jnp.einsum('fg,gzxy->fzxy', coupling, jnp.tanh(center), precision=highest)  45.2 us
    ppermute x1, waiting for transfers between devices, shards(): lax.ppermute(block_2, 'sim', forward)  40.9 us
    ppermute x16, starting transfers between devices, with_halo(): lax.ppermute(head, axis, [((i + 1) % count, i) for i in range(count)])  31.4 us
    all_gather x1, waiting for transfers between devices, shards(): incoming = lax.all_gather(projected, ('grp', 'gz'), axis=3, tiled=True)  17.9 us
    unnamed x5, waiting for transfers between devices  12.2 us
  transfers between devices with their start and end apart: 37, of which 37 were waited for; matrix products, arithmetic and copies ran while one was open for 8% of the time, Pallas kernels for 0%

profile of v1, /device:TPU:0, one launch (start us, length us, event | category | flops | bytes accessed | tf_op | source)
XLA Modules:
  0.0 473.9 jit_solution(1204799050187514679)
XLA Ops:
  7.2 2.8 copy.69
  10.3 3.1 collective-permute-start
  13.6 12.5 %collective-permute-done = f32[8,2,1,64]{2,0,3,1:T(8,128)S(1)} collective-permute-done((f32[8,2,1,64]{2,0,3,1:T(8,128)S(1)}, f32[8,2,1,64]{2,0,3,1:T(8,128)S(1)}, u32[]{:S(2)}, u32[]{:S(2)}) %collective-permute-start) | collective-permute-done | bytes 4128 | tf_op jit(solution)/shard_map/ppermute | solution.py:22
  26.1 10.4 %collective-permute-done.1 = f32[8,2,1,64]{2,0,3,1:T(8,128)S(1)} collective-permute-done((f32[8,2,1,64]{2,0,3,1:T(8,128)S(1)}, f32[8,2,1,64]{2,0,3,1:T(8,128)S(1)}, u32[]{:S(2)}, u32[]{:S(2)}) %collective-permute-start.1) | collective-permute-done | bytes 4128 | tf_op jit(solution)/shard_map/ppermute | solution.py:20
  36.6 3.4 collective-permute-start.2
  41.6 4.4 collective-permute-done.3
  46.1 5.2 %multiply_add_fusion.3 = (f32[8,2,512,64]{2,0,3,1:T(8,128)S(1)}, f32[8,2,512,64]{2,0,3,1:T(8,128)S(1)}) fusion(f32[8,2,512,64]{2,3,1,0:T(8,128)S(1)} %copy-done.4, f32[8,2,512,64]{2,3,1,0:T(8,128)S(1)} %tanh.24, f32[8,8]{1,0:T(8,128)S(1)} %copy-done.7, f32[8]{0:T(128)S(1)} %get-tuple-element.65, f32[8]{0:T(128)S(1)} %get-tuple-element.64, ...), kind=kOutput, calls=%fused_computation.163 | convolution fusion | flops 63963136 | bytes 12657248 | tf_op jit(solution)/shard_map/fg,gzxy->fzxy/dot_general | solution.py:41
  51.5 1.6 collective-permute-start.4
  53.6 12.5 %collective-permute-done.4 = f32[8,2,1,64]{2,0,3,1:T(8,128)S(1)} collective-permute-done((f32[8,2,1,64]{2,0,3,1:T(8,128)S(1)}, f32[8,2,1,64]{2,0,3,1:T(8,128)S(1)}, u32[]{:S(2)}, u32[]{:S(2)}) %collective-permute-start.4) | collective-permute-done | bytes 4128 | tf_op jit(solution)/shard_map/ppermute | solution.py:22
  66.1 5.6 %collective-permute-done.5 = f32[8,2,1,64]{2,0,3,1:T(8,128)S(1)} collective-permute-done((f32[8,2,1,64]{2,0,3,1:T(8,128)S(1)}, f32[8,2,1,64]{2,0,3,1:T(8,128)S(1)}, u32[]{:S(2)}, u32[]{:S(2)}) %collective-permute-start.5) | collective-permute-done | bytes 4128 | tf_op jit(solution)/shard_map/ppermute | solution.py:20
  71.9 4.1 collective-permute-start.6
  77.7 4.6 collective-permute-done.7
  82.3 4.5 multiply_add_fusion.2
  87.0 1.6 collective-permute-start.8
  89.1 12.5 %collective-permute-done.8 = f32[8,2,1,64]{2,0,3,1:T(8,128)S(1)} collective-permute-done((f32[8,2,1,64]{2,0,3,1:T(8,128)S(1)}, f32[8,2,1,64]{2,0,3,1:T(8,128)S(1)}, u32[]{:S(2)}, u32[]{:S(2)}) %collective-permute-start.8) | collective-permute-done | bytes 4128 | tf_op jit(solution)/shard_map/ppermute | solution.py:22
  101.6 5.6 %collective-permute-done.9 = f32[8,2,1,64]{2,0,3,1:T(8,128)S(1)} collective-permute-done((f32[8,2,1,64]{2,0,3,1:T(8,128)S(1)}, f32[8,2,1,64]{2,0,3,1:T(8,128)S(1)}, u32[]{:S(2)}, u32[]{:S(2)}) %collective-permute-start.9) | collective-permute-done | bytes 4128 | tf_op jit(solution)/shard_map/ppermute | solution.py:20
  107.3 2.7 collective-permute-start.10
  111.7 4.4 collective-permute-done.11
  116.1 4.9 %copy_add_fusion = (f32[8,2,512,64]{2,0,3,1:T(8,128)S(1)}, f32[8,2,512,64]{2,0,3,1:T(8,128)S(1)}) fusion(f32[8,2,512,64]{2,3,1,0:T(8,128)S(1)} %copy-done.4, f32[8,8]{1,0:T(8,128)S(1)} %copy-done.7, f32[8,2,512,64]{2,0,3,1:T(8,128)S(1)} %get-tuple-element.68, f32[8]{0:T(128)S(1)} %get-tuple-element.65, f32[8]{0:T(128)S(1)} %get-tuple-element.64, ...), kind=kOutput, calls=%fused_computation.217 | convolution fusion | flops 63438848 | bytes 10560096 | tf_op jit(solution)/shard_map/fg,gzxy->fzxy/dot_general | solution.py:41
  121.2 1.6 collective-permute-start.12
  123.3 12.5 %collective-permute-done.12 = f32[8,2,1,64]{2,0,3,1:T(8,128)S(1)} collective-permute-done((f32[8,2,1,64]{2,0,3,1:T(8,128)S(1)}, f32[8,2,1,64]{2,0,3,1:T(8,128)S(1)}, u32[]{:S(2)}, u32[]{:S(2)}) %collective-permute-start.12) | collective-permute-done | bytes 4128 | tf_op jit(solution)/shard_map/ppermute | solution.py:22
  135.8 5.6 %collective-permute-done.13 = f32[8,2,1,64]{2,0,3,1:T(8,128)S(1)} collective-permute-done((f32[8,2,1,64]{2,0,3,1:T(8,128)S(1)}, f32[8,2,1,64]{2,0,3,1:T(8,128)S(1)}, u32[]{:S(2)}, u32[]{:S(2)}) %collective-permute-start.13) | collective-permute-done | bytes 4128 | tf_op jit(solution)/shard_map/ppermute | solution.py:20
  144.5 4.6 collective-permute-done.15
  149.2 5.1 %fusion.34 = f32[8,2,512,64]{2,0,3,1:T(8,128)S(1)} fusion(f32[8,1,512,64]{2,0,3,1:T(8,128)S(1)} %get-tuple-element.51, f32[8,1,512,64]{2,0,3,1:T(8,128)S(1)} %get-tuple-element.50, f32[8,2,514,1]{2,0,3,1:T(8,128)S(1)} %collective-permute-done.14, f32[8,2,1,64]{2,0,3,1:T(8,128)S(1)} %collective-permute-done.12, f32[8,2,512,64]{2,0,3,1:T(8,128)S(1)} %get-tuple-element.70, ...), kind=kOutput, calls=%fused_computation.42 | convolution fusion | flops 66584576 | bytes 14754400 | tf_op jit(solution)/shard_map/fg,gzxy->fzxy/dot_general | solution.py:41
  154.5 1.6 collective-permute-start.16
  156.6 12.5 %collective-permute-done.16 = f32[8,2,1,64]{2,0,3,1:T(8,128)S(1)} collective-permute-done((f32[8,2,1,64]{2,0,3,1:T(8,128)S(1)}, f32[8,2,1,64]{2,0,3,1:T(8,128)S(1)}, u32[]{:S(2)}, u32[]{:S(2)}) %collective-permute-start.16) | collective-permute-done | bytes 4128 | tf_op jit(solution)/shard_map/ppermute | solution.py:22
  169.1 5.6 %collective-permute-done.17 = f32[8,2,1,64]{2,0,3,1:T(8,128)S(1)} collective-permute-done((f32[8,2,1,64]{2,0,3,1:T(8,128)S(1)}, f32[8,2,1,64]{2,0,3,1:T(8,128)S(1)}, u32[]{:S(2)}, u32[]{:S(2)}) %collective-permute-start.17) | collective-permute-done | bytes 4128 | tf_op jit(solution)/shard_map/ppermute | solution.py:20
  176.0 1.5 collective-permute-done.18
  177.5 4.4 collective-permute-done.19
  181.9 5.4 %multiply_add_fusion.1 = (f32[8,2,512,64]{2,0,3,1:T(8,128)S(1)}, f32[8,2,512,64]{2,0,3,1:T(8,128)}) fusion(f32[8,2,512,64]{2,0,3,1:T(8,128)S(1)} %fusion.34, f32[8,8]{1,0:T(8,128)S(1)} %copy-done.7, f32[8]{0:T(128)S(1)} %get-tuple-element.65, f32[8]{0:T(128)S(1)} %get-tuple-element.64, f32[8,2,1,64]{2,0,3,1:T(8,128)S(1)} %collective-permute-done.16, ...), kind=kOutput, calls=%fused_computation.153 | convolution fusion | flops 63963136 | bytes 8462944 | tf_op jit(solution)/shard_map/fg,gzxy->fzxy/dot_general | solution.py:41
  187.5 1.6 collective-permute-start.20
  189.6 12.5 %collective-permute-done.20 = f32[8,2,1,64]{2,0,3,1:T(8,128)S(1)} collective-permute-done((f32[8,2,1,64]{2,0,3,1:T(8,128)S(1)}, f32[8,2,1,64]{2,0,3,1:T(8,128)S(1)}, u32[]{:S(2)}, u32[]{:S(2)}) %collective-permute-start.20) | collective-permute-done | bytes 4128 | tf_op jit(solution)/shard_map/ppermute | solution.py:22
  202.1 5.6 %collective-permute-done.21 = f32[8,2,1,64]{2,0,3,1:T(8,128)S(1)} collective-permute-done((f32[8,2,1,64]{2,0,3,1:T(8,128)S(1)}, f32[8,2,1,64]{2,0,3,1:T(8,128)S(1)}, u32[]{:S(2)}, u32[]{:S(2)}) %collective-permute-start.21) | collective-permute-done | bytes 4128 | tf_op jit(solution)/shard_map/ppermute | solution.py:20
  210.7 4.4 collective-permute-done.23
  215.1 5.6 %multiply_add_fusion = (f32[8,2,512,64]{2,0,3,1:T(8,128)S(1)}, f32[8,2,512,64]{2,0,3,1:T(8,128)}) fusion(f32[8,2,512,64]{2,0,3,1:T(8,128)S(1)} %fusion.34, f32[8,8]{1,0:T(8,128)S(1)} %copy-done.7, f32[8,2,512,64]{2,0,3,1:T(8,128)S(1)} %get-tuple-element.72, f32[8]{0:T(128)S(1)} %get-tuple-element.65, f32[8]{0:T(128)S(1)} %get-tuple-element.64, ...), kind=kOutput, calls=%fused_computation.150 | convolution fusion | flops 63963136 | bytes 10560096 | tf_op jit(solution)/shard_map/fg,gzxy->fzxy/dot_general | solution.py:41
  220.9 1.6 collective-permute-start.24
  223.0 12.5 %collective-permute-done.24 = f32[8,2,1,64]{2,0,3,1:T(8,128)S(1)} collective-permute-done((f32[8,2,1,64]{2,0,3,1:T(8,128)S(1)}, f32[8,2,1,64]{2,0,3,1:T(8,128)S(1)}, u32[]{:S(2)}, u32[]{:S(2)}) %collective-permute-start.24) | collective-permute-done | bytes 4128 | tf_op jit(solution)/shard_map/ppermute | solution.py:22
  235.5 5.6 %collective-permute-done.25 = f32[8,2,1,64]{2,0,3,1:T(8,128)S(1)} collective-permute-done((f32[8,2,1,64]{2,0,3,1:T(8,128)S(1)}, f32[8,2,1,64]{2,0,3,1:T(8,128)S(1)}, u32[]{:S(2)}, u32[]{:S(2)}) %collective-permute-start.25) | collective-permute-done | bytes 4128 | tf_op jit(solution)/shard_map/ppermute | solution.py:20
  241.2 1.9 collective-permute-start.26
  244.8 4.8 %collective-permute-done.27 = f32[8,2,514,1]{2,0,3,1:T(8,128)S(1)} collective-permute-done((f32[8,2,514,1]{2,0,3,1:T(8,128)S(1)}, f32[8,2,514,1]{2,0,3,1:T(8,128)S(1)}, u32[]{:S(2)}, u32[]{:S(2)}) %collective-permute-start.27) | collective-permute-done | bytes 32928 | tf_op jit(solution)/shard_map/ppermute | solution.py:20
  249.7 5.6 %fusion.171 = (f32[8,2,512,64]{2,0,3,1:T(8,128)S(1)}, f32[8,2,512,64]{2,0,3,1:T(8,128)}) fusion(f32[8,2,512,64]{2,0,3,1:T(8,128)S(1)} %fusion.34, f32[8,8]{1,0:T(8,128)S(1)} %copy-done.7, f32[8,2,512,64]{2,0,3,1:T(8,128)S(1)} %get-tuple-element.74, f32[8]{0:T(128)S(1)} %get-tuple-element.65, f32[8]{0:T(128)S(1)} %get-tuple-element.64, ...), kind=kOutput, calls=%fused_computation.234 | convolution fusion | flops 63438848 | bytes 10560096 | tf_op jit(solution)/shard_map/fg,gzxy->fzxy/dot_general | solution.py:41
  256.6 1.5 collective-permute-start.28
  258.6 12.7 %collective-permute-done.28 = f32[8,2,1,64]{2,0,3,1:T(8,128)S(1)} collective-permute-done((f32[8,2,1,64]{2,0,3,1:T(8,128)}, f32[8,2,1,64]{2,0,3,1:T(8,128)S(1)}, u32[]{:S(2)}, u32[]{:S(2)}) %collective-permute-start.28) | collective-permute-done | bytes 4128 | tf_op jit(solution)/shard_map/ppermute | solution.py:22
  271.4 5.6 %collective-permute-done.29 = f32[8,2,1,64]{2,0,3,1:T(8,128)S(1)} collective-permute-done((f32[8,2,1,64]{2,0,3,1:T(8,128)}, f32[8,2,1,64]{2,0,3,1:T(8,128)S(1)}, u32[]{:S(2)}, u32[]{:S(2)}) %collective-permute-start.29) | collective-permute-done | bytes 4128 | tf_op jit(solution)/shard_map/ppermute | solution.py:20
  277.1 1.8 collective-permute-start.30
  280.5 4.5 collective-permute-done.31
  285.0 8.8 %fusion.69 = f32[8,2,512,64]{2,0,3,1:T(8,128)S(1)} fusion(f32[8,2,512,64]{2,0,3,1:T(8,128)S(1)} %copy-done.2, f32[8,1,512,64]{2,0,3,1:T(8,128)S(1)} %get-tuple-element.35, f32[8,1,512,64]{2,0,3,1:T(8,128)S(1)} %get-tuple-element.34, f32[8,2,514,1]{2,0,3,1:T(8,128)S(1)} %collective-permute-done.30, f32[8,2,1,64]{2,0,3,1:T(8,128)S(1)} %collective-permute-done.28, ...), kind=kOutput, calls=%fused_computation.77 | convolution fusion | flops 66584576 | bytes 14754400 | tf_op jit(solution)/shard_map/fg,gzxy->fzxy/dot_general | solution.py:41
  293.8 1.9 convolution_bitcast_fusion
  295.7 1.9 copy.90
  297.6 1.7 reshape.21
  299.4 12.1 %reduce-scatter.10.cloned.1.call-done = f32[64,1024]{1,0:T(8,128)} async-done(((f32[128,1024]{1,0:T(8,128)}), f32[64,1024]{1,0:T(8,128)}) %reduce-scatter.10.cloned.1.call-update) | async-done | bytes 262160
  314.7 1.6 broadcast_in_dim.2
  316.3 4.5 fusion.94
  320.8 40.9 %collective-permute-done.32 = f32[8,2,512,64]{2,0,3,1:T(8,128)} collective-permute-done((f32[8,2,512,64]{2,0,3,1:T(8,128)S(1)}, f32[8,2,512,64]{2,0,3,1:T(8,128)}, u32[]{:S(2)}, u32[]{:S(2)}) %collective-permute-start.32) | collective-permute-done | bytes 2097184 | tf_op jit(solution)/shard_map/ppermute | solution.py:68
  361.7 6.2 %fusion.102 = f32[512,1024]{0,1:T(8,128)} fusion(f32[512,1024]{0,1:T(8,128)} %fusion.94, s32[]{:T(128)S(6)} %select_n.26, f32[8,2,512,64]{2,0,3,1:T(8,128)} %collective-permute-done.32, f32[8,2,512,64]{2,0,3,1:T(8,128)S(1)} %fusion.69), kind=kOutput, calls=%fused_computation.170 | convolution fusion | flops 3221225472 | bytes 5242884 | tf_op jit(solution)/shard_map/fzxy,fzwy->xw/dot_general | solution.py:69
  368.2 2.5 copy.81
  370.7 17.9 %all-gather.2.cloned.1.call-done = f32[8,2,64,1024]{2,0,1,3:T(8,128)} async-done(((f32[8,2,64,64]{2,0,1,3:T(8,128)}), f32[8,2,64,1024]{2,0,1,3:T(8,128)}) %all-gather.2.cloned.1.call-update) | async-done | bytes 4194320 | tf_op jit(solution)/shard_map/all_gather | solution.py:89
  388.6 6.9 %copy.78 = f32[8,2,64,1024]{3,2,1,0:T(8,128)} copy(f32[8,2,64,1024]{2,0,1,3:T(8,128)} %all-gather.2.cloned.1.call-done) | data formatting | bytes 8388608 | tf_op jit(solution)/shard_map/all_gather | solution.py:89
  395.4 5.8 %convolution_bitcast_fusion.1 = f32[64,1024]{1,0:T(8,128)} fusion(f32[8,2,64,1024]{3,2,1,0:T(8,128)} %copy.78, f32[8,2,64,64]{3,1,0,2:T(2,128)S(1)} %bitcast.97), kind=kOutput, calls=%fused_computation.172 | convolution fusion | flops 805306368 | bytes 4718592 | tf_op jit(solution)/shard_map/fzry,fzrv->yv/dot_general | solution.py:90
  401.2 51.5 %reduce-scatter.6.cloned.1.call-done = f32[512,64]{0,1:T(8,128)} async-done(((f32[512,1024]{0,1:T(8,128)}), f32[512,64]{0,1:T(8,128)}) %reduce-scatter.6.cloned.1.call-update) | async-done | bytes 131088 | tf_op jit(solution)/shard_map/reduce_scatter | solution.py:82
  452.7 1.6 broadcast_multiply_fusion.1
  454.3 5.5 %fusion.108 = f32[8,2,64,8]{2,3,1,0:T(8,128)} fusion(f32[8,2,64,1024]{3,2,1,0:T(8,128)} %copy.78, bf16[1024,128]{1,0:T(8,128)(2,1)S(1)} %copy-done.5, s32[]{:T(128)S(6)} %select_n.28), kind=kOutput, calls=%fused_computation.174 | convolution fusion | flops 100663296 | bytes 4489220 | tf_op jit(solution)/shard_map/vs,fzrv->fzrs/dot_general | solution.py:91
  459.7 5.8 %reduce-scatter.8.cloned.1.call-done = f32[64,512]{1,0:T(8,128)} async-done(((f32[64,1024]{1,0:T(8,128)}), f32[64,512]{1,0:T(8,128)}) %reduce-scatter.8.cloned.1.call-update) | async-done | bytes 131088 | tf_op jit(solution)/shard_map/reduce_scatter | solution.py:92
  465.6 1.6 broadcast_multiply_fusion
  (85 shorter events, 26.1 us)
Async XLA Ops:
  7.2 286.7 %copy-start = (bf16[1024,128]{1,0:T(8,128)(2,1)S(1)}, bf16[1024,128]{1,0:T(8,128)(2,1)}, u32[]{:S(2)}) copy-start(bf16[1024,128]{1,0:T(8,128)(2,1)} %param.10) | copy-start | bytes 786436
  7.2 304.4 %reduce-scatter.10.cloned.1.call-start = ((), (), s32[]{:S(2)}) async-start(), calls=%async_computation.6 | async-start | bytes 786432
  10.3 15.8 %collective-permute-start = (f32[8,2,1,64]{2,0,3,1:T(8,128)S(1)}, f32[8,2,1,64]{2,0,3,1:T(8,128)S(1)}, u32[]{:S(2)}, u32[]{:S(2)}) collective-permute-start(f32[8,2,1,64]{2,0,3,1:T(8,128)S(1)} %get-tuple-element.61), channel_id=1, source_target_pairs={{16,0},{0,16},{17,1},{1,17},{18,2},{2,18},{19,3},{3,19},{20,4},{4,... | collective-permute-start | bytes 12296 | tf_op jit(solution)/shard_map/ppermute | solution.py:22
  13.3 23.2 %collective-permute-start.1 = (f32[8,2,1,64]{2,0,3,1:T(8,128)S(1)}, f32[8,2,1,64]{2,0,3,1:T(8,128)S(1)}, u32[]{:S(2)}, u32[]{:S(2)}) collective-permute-start(f32[8,2,1,64]{2,0,3,1:T(8,128)S(1)} %get-tuple-element.60), channel_id=1, source_target_pairs={{0,16},{16,0},{1,17},{17,1},{2,18},{18,2},{3,19},{19,3},{4,20},{20... | collective-permute-start | bytes 12296 | tf_op jit(solution)/shard_map/ppermute | solution.py:20
  13.6 26.4 %copy-start.6 = (f32[2,8]{1,0:T(2,128)S(1)}, f32[2,8]{1,0:T(2,128)}, u32[]{:S(2)}) copy-start(f32[2,8]{1,0:T(2,128)} %param.8) | copy-start | bytes 196
  13.6 26.4 %copy-start.4 = (f32[8,2,512,64]{2,3,1,0:T(8,128)S(1)}, f32[8,2,512,64]{2,3,1,0:T(8,128)}, u32[]{:S(2)}) copy-start(f32[8,2,512,64]{2,3,1,0:T(8,128)} %param.6) | copy-start | bytes 6291460
  36.6 5.1 %collective-permute-start.2 = (f32[8,2,514,1]{2,0,3,1:T(8,128)S(1)}, f32[8,2,514,1]{2,0,3,1:T(8,128)S(1)}, u32[]{:S(2)}, u32[]{:S(2)}) collective-permute-start(f32[8,2,514,1]{2,0,3,1:T(8,128)S(1)} %get-tuple-element.31), channel_id=1, source_target_pairs={{1,0},{2,1},{3,2},{4,3},{5,4},{6,5},{7,6},{8,7},{9,8},{10,9},{11,1... | collective-permute-start | bytes 98696 | tf_op jit(solution)/shard_map/ppermute | solution.py:22
  40.0 6.1 %collective-permute-start.3 = (f32[8,2,514,1]{2,0,3,1:T(8,128)S(1)}, f32[8,2,514,1]{2,0,3,1:T(8,128)S(1)}, u32[]{:S(2)}, u32[]{:S(2)}) collective-permute-start(f32[8,2,514,1]{2,0,3,1:T(8,128)S(1)} %get-tuple-element.30), channel_id=1, source_target_pairs={{0,1},{1,2},{2,3},{3,4},{4,5},{5,6},{6,7},{7,8},{8,9},{9,10},{10,1... | collective-permute-start | bytes 98696 | tf_op jit(solution)/shard_map/ppermute | solution.py:20
  40.0 6.1 %copy-start.7 = (f32[8,8]{1,0:T(8,128)S(1)}, f32[8,8]{1,0:T(8,128)}, u32[]{:S(2)}) copy-start(f32[8,8]{1,0:T(8,128)} %param.9) | copy-start | bytes 772
  40.0 6.1 %copy-start.8 = (f32[8]{0:T(128)S(1)}, f32[8]{0:T(128)}, u32[]{:S(2)}) copy-start(f32[8]{0:T(128)} %param.7) | copy-start | bytes 100
  51.5 14.6 %collective-permute-start.4 = (f32[8,2,1,64]{2,0,3,1:T(8,128)S(1)}, f32[8,2,1,64]{2,0,3,1:T(8,128)S(1)}, u32[]{:S(2)}, u32[]{:S(2)}) collective-permute-start(f32[8,2,1,64]{2,0,3,1:T(8,128)S(1)} %get-tuple-element.57), channel_id=1, source_target_pairs={{16,0},{0,16},{17,1},{1,17},{18,2},{2,18},{19,3},{3,19},{20,4},{4,... | collective-permute-start | bytes 12296 | tf_op jit(solution)/shard_map/ppermute | solution.py:22
  53.1 18.6 %collective-permute-start.5 = (f32[8,2,1,64]{2,0,3,1:T(8,128)S(1)}, f32[8,2,1,64]{2,0,3,1:T(8,128)S(1)}, u32[]{:S(2)}, u32[]{:S(2)}) collective-permute-start(f32[8,2,1,64]{2,0,3,1:T(8,128)S(1)} %get-tuple-element.56), channel_id=1, source_target_pairs={{0,16},{16,0},{1,17},{17,1},{2,18},{18,2},{3,19},{19,3},{4,20},{20... | collective-permute-start | bytes 12296 | tf_op jit(solution)/shard_map/ppermute | solution.py:20
  71.9 5.8 %collective-permute-start.6 = (f32[8,2,514,1]{2,0,3,1:T(8,128)S(1)}, f32[8,2,514,1]{2,0,3,1:T(8,128)S(1)}, u32[]{:S(2)}, u32[]{:S(2)}) collective-permute-start(f32[8,2,514,1]{2,0,3,1:T(8,128)S(1)} %get-tuple-element.29), channel_id=1, source_target_pairs={{1,0},{2,1},{3,2},{4,3},{5,4},{6,5},{7,6},{8,7},{9,8},{10,9},{11,1... | collective-permute-start | bytes 98696 | tf_op jit(solution)/shard_map/ppermute | solution.py:22
  76.0 6.3 %collective-permute-start.7 = (f32[8,2,514,1]{2,0,3,1:T(8,128)S(1)}, f32[8,2,514,1]{2,0,3,1:T(8,128)S(1)}, u32[]{:S(2)}, u32[]{:S(2)}) collective-permute-start(f32[8,2,514,1]{2,0,3,1:T(8,128)S(1)} %get-tuple-element.28), channel_id=1, source_target_pairs={{0,1},{1,2},{2,3},{3,4},{4,5},{5,6},{6,7},{7,8},{8,9},{9,10},{10,1... | collective-permute-start | bytes 98696 | tf_op jit(solution)/shard_map/ppermute | solution.py:20
  87.0 14.6 %collective-permute-start.8 = (f32[8,2,1,64]{2,0,3,1:T(8,128)S(1)}, f32[8,2,1,64]{2,0,3,1:T(8,128)S(1)}, u32[]{:S(2)}, u32[]{:S(2)}) collective-permute-start(f32[8,2,1,64]{2,0,3,1:T(8,128)S(1)} %get-tuple-element.53), channel_id=1, source_target_pairs={{16,0},{0,16},{17,1},{1,17},{18,2},{2,18},{19,3},{3,19},{20,4},{4,... | collective-permute-start | bytes 12296 | tf_op jit(solution)/shard_map/ppermute | solution.py:22
  88.6 18.6 %collective-permute-start.9 = (f32[8,2,1,64]{2,0,3,1:T(8,128)S(1)}, f32[8,2,1,64]{2,0,3,1:T(8,128)S(1)}, u32[]{:S(2)}, u32[]{:S(2)}) collective-permute-start(f32[8,2,1,64]{2,0,3,1:T(8,128)S(1)} %get-tuple-element.52), channel_id=1, source_target_pairs={{0,16},{16,0},{1,17},{17,1},{2,18},{18,2},{3,19},{19,3},{4,20},{20... | collective-permute-start | bytes 12296 | tf_op jit(solution)/shard_map/ppermute | solution.py:20
  107.3 4.3 collective-permute-start.10
  110.0 6.1 %collective-permute-start.11 = (f32[8,2,514,1]{2,0,3,1:T(8,128)S(1)}, f32[8,2,514,1]{2,0,3,1:T(8,128)S(1)}, u32[]{:S(2)}, u32[]{:S(2)}) collective-permute-start(f32[8,2,514,1]{2,0,3,1:T(8,128)S(1)} %get-tuple-element.26), channel_id=1, source_target_pairs={{0,1},{1,2},{2,3},{3,4},{4,5},{5,6},{6,7},{7,8},{8,9},{9,10},{10,1... | collective-permute-start | bytes 98696 | tf_op jit(solution)/shard_map/ppermute | solution.py:20
  121.2 14.6 %collective-permute-start.12 = (f32[8,2,1,64]{2,0,3,1:T(8,128)S(1)}, f32[8,2,1,64]{2,0,3,1:T(8,128)S(1)}, u32[]{:S(2)}, u32[]{:S(2)}) collective-permute-start(f32[8,2,1,64]{2,0,3,1:T(8,128)S(1)} %get-tuple-element.49), channel_id=1, source_target_pairs={{16,0},{0,16},{17,1},{1,17},{18,2},{2,18},{19,3},{3,19},{20,4},{4,... | collective-permute-start | bytes 12296 | tf_op jit(solution)/shard_map/ppermute | solution.py:22
  122.8 18.6 %collective-permute-start.13 = (f32[8,2,1,64]{2,0,3,1:T(8,128)S(1)}, f32[8,2,1,64]{2,0,3,1:T(8,128)S(1)}, u32[]{:S(2)}, u32[]{:S(2)}) collective-permute-start(f32[8,2,1,64]{2,0,3,1:T(8,128)S(1)} %get-tuple-element.48), channel_id=1, source_target_pairs={{0,16},{16,0},{1,17},{17,1},{2,18},{18,2},{3,19},{19,3},{4,20},{20... | collective-permute-start | bytes 12296 | tf_op jit(solution)/shard_map/ppermute | solution.py:20
  141.5 3.0 collective-permute-start.14
  142.9 6.3 %collective-permute-start.15 = (f32[8,2,514,1]{2,0,3,1:T(8,128)S(1)}, f32[8,2,514,1]{2,0,3,1:T(8,128)S(1)}, u32[]{:S(2)}, u32[]{:S(2)}) collective-permute-start(f32[8,2,514,1]{2,0,3,1:T(8,128)S(1)} %get-tuple-element.24), channel_id=1, source_target_pairs={{0,1},{1,2},{2,3},{3,4},{4,5},{5,6},{6,7},{7,8},{8,9},{9,10},{10,1... | collective-permute-start | bytes 98696 | tf_op jit(solution)/shard_map/ppermute | solution.py:20
  154.3 95.4 %copy-start.1 = (f32[8,2,512,64]{2,0,3,1:T(8,128)}, f32[8,2,512,64]{2,0,3,1:T(8,128)S(1)}, u32[]{:S(2)}) copy-start(f32[8,2,512,64]{2,0,3,1:T(8,128)S(1)} %fusion.34) | copy-start | bytes 6291460
  154.5 14.6 %collective-permute-start.16 = (f32[8,2,1,64]{2,0,3,1:T(8,128)S(1)}, f32[8,2,1,64]{2,0,3,1:T(8,128)S(1)}, u32[]{:S(2)}, u32[]{:S(2)}) collective-permute-start(f32[8,2,1,64]{2,0,3,1:T(8,128)S(1)} %get-tuple-element.45), channel_id=1, source_target_pairs={{16,0},{0,16},{17,1},{1,17},{18,2},{2,18},{19,3},{3,19},{20,4},{4,... | collective-permute-start | bytes 12296 | tf_op jit(solution)/shard_map/ppermute | solution.py:22
  156.1 18.6 %collective-permute-start.17 = (f32[8,2,1,64]{2,0,3,1:T(8,128)S(1)}, f32[8,2,1,64]{2,0,3,1:T(8,128)S(1)}, u32[]{:S(2)}, u32[]{:S(2)}) collective-permute-start(f32[8,2,1,64]{2,0,3,1:T(8,128)S(1)} %get-tuple-element.44), channel_id=1, source_target_pairs={{0,16},{16,0},{1,17},{17,1},{2,18},{18,2},{3,19},{19,3},{4,20},{20... | collective-permute-start | bytes 12296 | tf_op jit(solution)/shard_map/ppermute | solution.py:20
  174.8 2.6 collective-permute-start.18
  175.8 6.1 %collective-permute-start.19 = (f32[8,2,514,1]{2,0,3,1:T(8,128)S(1)}, f32[8,2,514,1]{2,0,3,1:T(8,128)S(1)}, u32[]{:S(2)}, u32[]{:S(2)}) collective-permute-start(f32[8,2,514,1]{2,0,3,1:T(8,128)S(1)} %get-tuple-element.22), channel_id=1, source_target_pairs={{0,1},{1,2},{2,3},{3,4},{4,5},{5,6},{6,7},{7,8},{8,9},{9,10},{10,1... | collective-permute-start | bytes 98696 | tf_op jit(solution)/shard_map/ppermute | solution.py:20
  187.5 14.6 %collective-permute-start.20 = (f32[8,2,1,64]{2,0,3,1:T(8,128)S(1)}, f32[8,2,1,64]{2,0,3,1:T(8,128)S(1)}, u32[]{:S(2)}, u32[]{:S(2)}) collective-permute-start(f32[8,2,1,64]{2,0,3,1:T(8,128)S(1)} %get-tuple-element.41), channel_id=1, source_target_pairs={{16,0},{0,16},{17,1},{1,17},{18,2},{2,18},{19,3},{3,19},{20,4},{4,... | collective-permute-start | bytes 12296 | tf_op jit(solution)/shard_map/ppermute | solution.py:22
  189.1 18.6 %collective-permute-start.21 = (f32[8,2,1,64]{2,0,3,1:T(8,128)S(1)}, f32[8,2,1,64]{2,0,3,1:T(8,128)S(1)}, u32[]{:S(2)}, u32[]{:S(2)}) collective-permute-start(f32[8,2,1,64]{2,0,3,1:T(8,128)S(1)} %get-tuple-element.40), channel_id=1, source_target_pairs={{0,16},{16,0},{1,17},{17,1},{2,18},{18,2},{3,19},{19,3},{4,20},{20... | collective-permute-start | bytes 12296 | tf_op jit(solution)/shard_map/ppermute | solution.py:20
  207.8 2.8 collective-permute-start.22
  209.0 6.1 %collective-permute-start.23 = (f32[8,2,514,1]{2,0,3,1:T(8,128)S(1)}, f32[8,2,514,1]{2,0,3,1:T(8,128)S(1)}, u32[]{:S(2)}, u32[]{:S(2)}) collective-permute-start(f32[8,2,514,1]{2,0,3,1:T(8,128)S(1)} %get-tuple-element.20), channel_id=1, source_target_pairs={{0,1},{1,2},{2,3},{3,4},{4,5},{5,6},{6,7},{7,8},{8,9},{9,10},{10,1... | collective-permute-start | bytes 98696 | tf_op jit(solution)/shard_map/ppermute | solution.py:20
  220.9 14.6 %collective-permute-start.24 = (f32[8,2,1,64]{2,0,3,1:T(8,128)S(1)}, f32[8,2,1,64]{2,0,3,1:T(8,128)S(1)}, u32[]{:S(2)}, u32[]{:S(2)}) collective-permute-start(f32[8,2,1,64]{2,0,3,1:T(8,128)S(1)} %get-tuple-element.37), channel_id=1, source_target_pairs={{16,0},{0,16},{17,1},{1,17},{18,2},{2,18},{19,3},{3,19},{20,4},{4,... | collective-permute-start | bytes 12296 | tf_op jit(solution)/shard_map/ppermute | solution.py:22
  222.5 18.6 %collective-permute-start.25 = (f32[8,2,1,64]{2,0,3,1:T(8,128)S(1)}, f32[8,2,1,64]{2,0,3,1:T(8,128)S(1)}, u32[]{:S(2)}, u32[]{:S(2)}) collective-permute-start(f32[8,2,1,64]{2,0,3,1:T(8,128)S(1)} %get-tuple-element.36), channel_id=1, source_target_pairs={{0,16},{16,0},{1,17},{17,1},{2,18},{18,2},{3,19},{19,3},{4,20},{20... | collective-permute-start | bytes 12296 | tf_op jit(solution)/shard_map/ppermute | solution.py:20
  241.2 3.6 collective-permute-start.26
  243.2 6.5 %collective-permute-start.27 = (f32[8,2,514,1]{2,0,3,1:T(8,128)S(1)}, f32[8,2,514,1]{2,0,3,1:T(8,128)S(1)}, u32[]{:S(2)}, u32[]{:S(2)}) collective-permute-start(f32[8,2,514,1]{2,0,3,1:T(8,128)S(1)} %get-tuple-element.18), channel_id=1, source_target_pairs={{0,1},{1,2},{2,3},{3,4},{4,5},{5,6},{6,7},{7,8},{8,9},{9,10},{10,1... | collective-permute-start | bytes 98696 | tf_op jit(solution)/shard_map/ppermute | solution.py:20
  255.3 23.6 %copy-start.3 = (f32[8,2,512,64]{2,0,3,1:T(8,128)}, f32[8,2,512,64]{2,0,3,1:T(8,128)S(1)}, u32[]{:S(2)}) copy-start(f32[8,2,512,64]{2,0,3,1:T(8,128)S(1)} %get-tuple-element.76) | copy-start | bytes 6291460
  256.6 14.8 %collective-permute-start.28 = (f32[8,2,1,64]{2,0,3,1:T(8,128)}, f32[8,2,1,64]{2,0,3,1:T(8,128)S(1)}, u32[]{:S(2)}, u32[]{:S(2)}) collective-permute-start(f32[8,2,1,64]{2,0,3,1:T(8,128)} %get-tuple-element.33), channel_id=1, source_target_pairs={{16,0},{0,16},{17,1},{1,17},{18,2},{2,18},{19,3},{3,19},{20,4},{4,... | collective-permute-start | bytes 12296 | tf_op jit(solution)/shard_map/ppermute | solution.py:22
  258.1 18.9 %collective-permute-start.29 = (f32[8,2,1,64]{2,0,3,1:T(8,128)}, f32[8,2,1,64]{2,0,3,1:T(8,128)S(1)}, u32[]{:S(2)}, u32[]{:S(2)}) collective-permute-start(f32[8,2,1,64]{2,0,3,1:T(8,128)} %get-tuple-element.32), channel_id=1, source_target_pairs={{0,16},{16,0},{1,17},{17,1},{2,18},{18,2},{3,19},{19,3},{4,20},{20... | collective-permute-start | bytes 12296 | tf_op jit(solution)/shard_map/ppermute | solution.py:20
  277.0 8.0 %copy-start.10 = (f32[8,2,512,64]{2,0,3,1:T(8,128)S(1)}, f32[8,2,512,64]{2,0,3,1:T(8,128)}, u32[]{:S(2)}) copy-start(f32[8,2,512,64]{2,0,3,1:T(8,128)} %get-tuple-element.75) | copy-start | bytes 6291460
  277.1 3.4 collective-permute-start.30
  278.8 6.1 %copy-start.2 = (f32[8,2,512,64]{2,0,3,1:T(8,128)S(1)}, f32[8,2,512,64]{2,0,3,1:T(8,128)}, u32[]{:S(2)}) copy-start(f32[8,2,512,64]{2,0,3,1:T(8,128)} %copy-done.1) | copy-start | bytes 6291460
  278.9 6.1 %copy-start.9 = (f32[8,2,512,64]{2,0,3,1:T(8,128)S(1)}, f32[8,2,512,64]{2,0,3,1:T(8,128)}, u32[]{:S(2)}) copy-start(f32[8,2,512,64]{2,0,3,1:T(8,128)} %get-tuple-element.73) | copy-start | bytes 6291460
  278.9 6.1 %collective-permute-start.31 = (f32[8,2,514,1]{2,0,3,1:T(8,128)S(1)}, f32[8,2,514,1]{2,0,3,1:T(8,128)S(1)}, u32[]{:S(2)}, u32[]{:S(2)}) collective-permute-start(f32[8,2,514,1]{2,0,3,1:T(8,128)S(1)} %get-tuple-element.16), channel_id=1, source_target_pairs={{0,1},{1,2},{2,3},{3,4},{4,5},{5,6},{6,7},{7,8},{8,9},{9,10},{10,1... | collective-permute-start | bytes 98696 | tf_op jit(solution)/shard_map/ppermute | solution.py:20
  299.4 89.2 %all-gather.2.cloned.1.call-start = ((), (), s32[]{:S(2)}) async-start(), calls=%async_computation.4 | async-start | bytes 8912896 | tf_op jit(solution)/shard_map/all_gather | solution.py:89
  314.1 138.6 %reduce-scatter.6.cloned.1.call-start = ((), (), s32[]{:S(2)}) async-start(), calls=%async_computation.3 | async-start | bytes 2228224 | tf_op jit(solution)/shard_map/reduce_scatter | solution.py:82
  314.3 47.4 %collective-permute-start.32 = (f32[8,2,512,64]{2,0,3,1:T(8,128)S(1)}, f32[8,2,512,64]{2,0,3,1:T(8,128)}, u32[]{:S(2)}, u32[]{:S(2)}) collective-permute-start(f32[8,2,512,64]{2,0,3,1:T(8,128)S(1)} %fusion.69), channel_id=1, source_target_pairs={{0,16},{16,0},{1,17},{17,1},{2,18},{18,2},{3,19},{19,3},{4,20},{20... | collective-permute-start | bytes 6291464 | tf_op jit(solution)/shard_map/ppermute | solution.py:68
  367.9 97.7 %reduce-scatter.8.cloned.1.call-start = ((), (), s32[]{:S(2)}) async-start(), calls=%async_computation.5 | async-start | bytes 393216 | tf_op jit(solution)/shard_map/reduce_scatter | solution.py:92
  395.4 58.9 %copy-start.5 = (bf16[1024,128]{1,0:T(8,128)(2,1)S(1)}, bf16[1024,128]{1,0:T(8,128)(2,1)}, u32[]{:S(2)}) copy-start(bf16[1024,128]{1,0:T(8,128)(2,1)} %param.11) | copy-start | bytes 786436
Sparse Core Ops, SparseCore 0:
  299.5 11.9 reduce-scatter.9
  314.2 74.2 all-gather.1
  392.3 60.3 reduce-scatter.5
  454.8 10.7 reduce-scatter.7
